TPU v7x, 256 devices: a whole 4x4x8 slice. The times are simulated.
256 devices in a mesh: term: 8 (over z), sec: 32 (over y, x, core).
Axes of the slice: x: 4, y: 4, z: 8, core: 2. Of those that a mesh axis runs over, the one named last changes fastest.
Arguments:
- start_vectors: bfloat16 [2, 64, 256, 256], P(None, 'sec'), may hold values from -6 to 6
- left_env: bfloat16 [32, 64, 256, 256], P('term', 'sec'), may hold values from -0.375 to 0.375
- right_env: bfloat16 [32, 64, 256, 256], P('term', 'sec'), may hold values from -0.375 to 0.375
- term_shift: int32 [32], P('term'), may hold values from -1 to 1
- precond: float32 [64, 256, 256], P('sec'), may hold values from 0.25 to 4
- block_dims: int32 [64], P('sec'), may hold values from 1 to 256, 8192 in all
Outputs:
- vector: float32 [2, 64, 256, 256], P(None, 'sec', 'term')
- energy: float32 [2], replicated
Inputs may be any that keep to these rules, and one draw needn't show every extreme that they name: `block_dims`: one block has exactly 256 live states.
All inputs are finite; a program needn't handle non-finite values.
Results may differ from a plain program's by a relative error of at most 0.0036.
Values may be sent and summed in bfloat16 or wider, within the bound.
No kernel may reach another device: no remote copies, remote signals or barrier semaphores. Data moves between devices by JAX's collectives and lax.ppermute only.
A program may use at most 64 MiB of HBM per device.

v0:
```python
import functools

import jax
import jax.numpy as jnp
from jax import lax
from jax.experimental import pallas as pl
from jax.experimental.pallas import tpu as pltpu
from jax.sharding import PartitionSpec as P


BF = jnp.bfloat16
F32 = jnp.float32
PAIRS = [(i, j) for i in range(4) for j in range(i, 4)]
PLAIN = [(0, 0), (0, 1), (1, 1), (0, 2), (0, 3), (1, 2), (1, 3)]
EXTRA = 8


def fold(product):
    rows, cols = product.shape
    tile = jnp.sum(product.reshape(rows // 8, 8, cols), axis=0)
    return sum(tile[:, i : i + 128] for i in range(0, cols, 128))


def slot_of(core_ref, shift_ref, k, b):
    at, core = b + shift_ref[k], core_ref[0]
    return jnp.where(at < 0, 3 - core, jnp.where(at > 1, 2 + core, at))


def apply_kernel(count, core_ref, shift_ref, x_ref, right_ref, left_ref, *refs):
    field_refs, paired_refs, rest = refs[: count[0]], refs[count[0] : sum(count)], refs[sum(count) :]
    out_ref, z_ref = rest[0], rest[-1]
    vecs, _, states, _ = x_ref.shape
    terms, blocks = left_ref.shape[:2]
    for k in range(terms):
        for b in range(blocks):
            slot = slot_of(core_ref, shift_ref, k, b)
            x = x_ref[:, slot].reshape(vecs * states, states)
            z = lax.dot_general(
                x, right_ref[k, slot], (((1,), (1,)), ((), ())), preferred_element_type=F32
            ).astype(BF)
            for u in range(vecs):
                z_ref[b, pl.ds(k * states, states), pl.ds(u * states, states)] = z[
                    u * states : (u + 1) * states
                ]
    if sum(count):
        dot_ref = rest[-2]
        dot_ref[...] = jnp.zeros_like(dot_ref)
    for b in range(blocks):
        wide = jnp.concatenate([left_ref[k, b] for k in range(terms)], axis=1)
        acc = jnp.dot(wide, z_ref[b], preferred_element_type=F32)
        for u in range(vecs):
            part = acc[:, u * states : (u + 1) * states]
            if not sum(count):
                groups, share = out_ref.shape[0], out_ref.shape[3]
                out_ref[:, u, b] = part.reshape(groups, share, states).astype(out_ref.dtype)
            elif len(rest) == 3:
                out_ref[u, b] = part.astype(out_ref.dtype)
            products = [part * f[u, b].astype(F32) for f in field_refs]
            products += [x_ref[u, b].astype(F32) * f[u, b].astype(F32) for f in paired_refs]
            for i, product in enumerate(products):
                dot_ref[i, u] = dot_ref[i, u] + fold(product)


def settle_kernel(factor, got_ref, mask_ref, *refs):
    h_ref, body_ref = refs[-2:]
    groups, vecs, blocks, share, states = got_ref.shape
    row = jnp.zeros((1, 128), F32)
    lane = lax.broadcasted_iota(jnp.int32, (1, 128), 1)
    for u in range(vecs):
        tiles = [jnp.zeros((8, 128), F32) for _ in range(8)]
        for b in range(blocks):
            h = got_ref[0, u, b].astype(F32)
            for t in range(1, groups):
                h = h + got_ref[t, u, b].astype(F32)
            h = h * mask_ref[b]
            h_ref[u, b] = h
            small = h.astype(BF)
            for t in range(groups):
                body_ref[t, pl.ds((u * blocks + b) * share, share), :] = small
            if len(refs) == 4:
                v, m = refs[0][u, b].astype(F32), refs[1][b]
                mv, mh = m * v, m * h
                products = [v * v, v * h, v * mv, v * mh, h * mh, mv * mv, mv * mh, mh * mh]
                tiles = [x + fold(y) for x, y in zip(tiles, products)]
        if len(refs) == 4:
            for i, tile in enumerate(tiles):
                row = row + jnp.where(lane == i * vecs + u, jnp.sum(tile) * factor, 0.0)
    if len(refs) == 4:
        high = row.astype(BF).astype(F32)
        middle = (row - high).astype(BF).astype(F32)
        low = row - high - middle
        index = lax.broadcasted_iota(jnp.int32, (EXTRA, 128), 0)
        tile = jnp.where(index == 0, high, jnp.where(index == 1, middle, jnp.where(index == 2, low, 0.0)))
        tile = tile.astype(BF)
        for t in range(groups):
            body_ref[t, pl.ds(vecs * blocks * share, EXTRA), pl.ds(0, 128)] = tile
            body_ref[t, pl.ds(vecs * blocks * share, EXTRA), pl.ds(128, states - 128)] = jnp.zeros(
                (EXTRA, states - 128), BF
            )


def block_of(got_ref, u, b, blocks, share):
    groups, _, states = got_ref.shape
    start = (u * blocks + b) * share
    if not isinstance(start, int):
        start = pl.multiple_of(start, share)
    return got_ref[:, pl.ds(start, share), :].reshape(groups * share, states)


def unpack_kernel(core_ref, got_ref, *refs):
    inner_ref, outer_ref = refs[1:3] if len(refs) == 4 else refs
    groups, _, states = got_ref.shape
    vecs, share = 2, states // groups
    core = core_ref[0]
    for ref, b in ((inner_ref, 1 - core), (outer_ref, core)):
        for u in range(vecs):
            ref[u] = block_of(got_ref, u, b, 2, share)
        if len(refs) == 4:
            ref[vecs] = refs[0][b].astype(BF)
    if len(refs) == 4:
        tile = jnp.zeros((EXTRA, 128), F32)
        for t in range(groups):
            tile = tile + got_ref[t, pl.ds(vecs * 2 * share, EXTRA), pl.ds(0, 128)].astype(F32)
        row_ref = refs[3]
        row_ref[...] = jnp.broadcast_to(jnp.sum(tile, axis=0, keepdims=True)[None], row_ref.shape)


def slot_blocks(own_ref, core_ref, chip_ref, u, share):
    own = [block_of(own_ref, u, b, 2, share) for b in range(2)]
    return own + [core_ref[u], chip_ref[u]]


def pick(row, i, vecs):
    return row if i == 0 else pltpu.roll(row, 128 - i * vecs, 1)


def lane_of(row, u):
    lane = lax.broadcasted_iota(jnp.int32, row.shape, 1)
    return jnp.sum(jnp.where(lane == u, row, 0.0), axis=1, keepdims=True)


def weight_of(own_ref, core_ref, chip_ref, i):
    if i < 2:
        return own_ref[i]
    ref = (core_ref, chip_ref)[i - 2]
    return ref[ref.shape[0] - 1].astype(F32)


def form_kernel(row_ref, got_ref, core_ref, chip_ref, start_ref, pre_ref, pre_core, pre_chip, dir_ref, mdir_ref, coef_ref):
    vecs, slots, states, _ = dir_ref.shape
    share = states // got_ref.shape[0]
    row = row_ref[0]
    for i in range(1, row_ref.shape[0]):
        row = row + row_ref[i]
    total = [pick(row, i, vecs) for i in range(8)]
    scale = 1.0 / jnp.sqrt(total[0] + 1e-06)
    vv, vh, vmv, vmh, hmh, mvmv, mvmh, mhmh = [x * (scale * scale) for x in total]
    correlation = vmh - vh * vmv
    square = mhmh - 2.0 * vh * mvmh + vh * vh * mvmv
    square = square - 2.0 * correlation * (vmh - vh * vmv) + correlation * correlation * vv
    norm = jnp.sqrt(jnp.maximum(square, 0.0) + 1e-06)
    coupling = (hmh - vh * vmh - correlation * vh) / norm
    alpha = scale / norm
    for j, x in enumerate([vh, correlation, alpha, scale, coupling, norm]):
        coef_ref[j] = jnp.broadcast_to(x, coef_ref.shape[1:])
    for u in range(vecs):
        ray, corr, mult = [lane_of(x[0:1], u) for x in (vh, correlation, alpha)]
        hs = slot_blocks(got_ref, core_ref, chip_ref, u, share)
        for i in range(slots):
            m = weight_of(pre_ref, pre_core, pre_chip, i)
            v = start_ref[u, i].astype(F32)
            raw = m * (hs[i].astype(F32) - ray * v) - corr * v
            small = (raw * mult).astype(BF)
            dir_ref[u, i] = small
            mdir_ref[u, i] = (m * small.astype(F32)).astype(BF)


def lift_kernel(got_ref, core_ref, chip_ref, pre_ref, pre_core, pre_chip, out_ref):
    vecs, slots, states, _ = out_ref.shape
    share = states // got_ref.shape[0]
    for u in range(vecs):
        hs = slot_blocks(got_ref, core_ref, chip_ref, u, share)
        for i in range(slots):
            m = weight_of(pre_ref, pre_core, pre_chip, i)
            out_ref[u, i] = (m * hs[i].astype(F32)).astype(BF)


def lift_start_kernel(start_ref, pre_ref, pre_core, pre_chip, out_ref):
    vecs, slots = out_ref.shape[:2]
    for u in range(vecs):
        for i in range(slots):
            m = weight_of(pre_ref, pre_core, pre_chip, i)
            out_ref[u, i] = (m * start_ref[u, i].astype(F32)).astype(BF)


def gram_kernel(coef_ref, start_ref, h_ref, hd_ref, pre_ref, dot_ref, dir_ref):
    vecs, blocks = h_ref.shape[:2]
    for u in range(vecs):
        rayleigh, correlation, alpha, scale = [lane_of(coef_ref[j, 0:1], u) for j in range(4)]
        for b in range(blocks):
            m = pre_ref[b]
            v, h = start_ref[u, b].astype(F32), h_ref[u, b]
            d = (m * (h - rayleigh * v) - correlation * v) * alpha
            dir_ref[u, b] = d
            basis = [v * scale, d, h * scale, hd_ref[u, b]]
            lifted = [m * x for x in basis]
            products = [basis[i] * basis[j] for i, j in PLAIN]
            products += [basis[i] * lifted[j] for i, j in PAIRS]
            products += [lifted[i] * lifted[j] for i, j in PAIRS]
            for i, product in enumerate(products):
                tile = fold(product)
                dot_ref[i, u] = tile if b == 0 else dot_ref[i, u] + tile


def tally_kernel(factor, *refs):
    out_ref = refs[-1]
    lines = []
    for ref in refs[:-1]:
        for i in range(ref.shape[0]):
            lines += [jnp.sum(ref[i, u], axis=0, keepdims=True) for u in range(ref.shape[1])]
    lines.append(jnp.zeros((128 - len(lines), 128), F32))
    table = jnp.concatenate(lines, axis=0)
    row = lax.dot_general(
        jnp.ones((8, 128), F32),
        table,
        (((1,), (1,)), ((), ())),
        precision=lax.Precision.HIGHEST,
        preferred_element_type=F32,
    )
    out_ref[...] = jnp.broadcast_to((row[0:1] * factor)[None], out_ref.shape)


def pack_kernel(core_ref, dims_hbm, start_ref, right_ref, out_ref, dims_ref, raw, sem):
    terms, vecs = right_ref.shape[0], start_ref.shape[0]
    states = out_ref.shape[1]
    b = core_ref[0]
    copies = [pltpu.make_async_copy(dims_hbm, dims_ref, sem.at[0])]
    copies += [pltpu.make_async_copy(start_ref.at[u, b], raw.at[u], sem.at[1 + u]) for u in range(vecs)]
    for k in range(terms):
        copies.append(pltpu.make_async_copy(right_ref.at[k, b], out_ref.at[k], sem.at[1 + vecs + k]))
    for copy in copies:
        copy.start()
    for copy in copies[: vecs + 1]:
        copy.wait()
    row = lax.broadcasted_iota(jnp.int32, (states, states), 0)
    col = lax.broadcasted_iota(jnp.int32, (states, states), 1)
    keep = (row < dims_ref[b]) & (col < dims_ref[b])
    for u in range(vecs):
        out_ref[terms + u] = jnp.where(keep, raw[u].astype(F32), 0.0).astype(BF)
    for copy in copies[vecs + 1 :]:
        copy.wait()


def load_kernel(core_ref, term_ref, dims_ref, shift_ref, start_ref, left_ref, right_ref, pre_ref, own_ref, left_out, right_out, mask_out, pre_out, vec_out, near_out, raw, weights, sem):
    vecs, blocks, states, _ = own_ref.shape
    terms = left_ref.shape[0]
    share = vec_out.shape[2]
    core = core_ref[0]
    first = pltpu.make_async_copy(start_ref, raw, sem.at[0])
    second = pltpu.make_async_copy(pre_ref, weights, sem.at[1])
    rest = []
    for k in range(terms):
        rest.append(pltpu.make_async_copy(right_ref.at[k, 1 - core], near_out.at[k], sem.at[2 + 3 * k]))
        rest.append(pltpu.make_async_copy(right_ref.at[k], right_out.at[k], sem.at[3 + 3 * k]))
        rest.append(pltpu.make_async_copy(left_ref.at[k], left_out.at[k], sem.at[4 + 3 * k]))
    for copy in [first, second] + rest:
        copy.start()
    here = pl.ds(pl.multiple_of(term_ref[0] * share, share), share)
    row = lax.broadcasted_iota(jnp.int32, (states, states), 0)
    col = lax.broadcasted_iota(jnp.int32, (states, states), 1)
    first.wait()
    for b in range(blocks):
        keep = (row < dims_ref[b]) & (col < dims_ref[b])
        for u in range(vecs):
            own_ref[u, b] = jnp.where(keep, raw[u, b].astype(F32), 0.0).astype(BF)
            vec_out[u, b] = own_ref[u, b, here, :]
        low = row[:share] + term_ref[0] * share
        mask_out[b] = jnp.where((low < dims_ref[b]) & (col[:share] < dims_ref[b]), 1.0, 0.0)
    second.wait()
    for b in range(blocks):
        pre_out[b] = weights[b, here, :]
    for u in range(vecs):
        near_out[terms + u] = own_ref[u, 1 - core]
    for copy in rest:
        copy.wait()


def form(table, left, right):
    result = None
    for i, x in left:
        for j, y in right:
            term = x * y * table[(min(i, j), max(i, j))]
            result = term if result is None else result + term
    return result


def lowest(rayleigh, curvature, coupling):
    half = 0.5 * (rayleigh - curvature)
    energy = 0.5 * (rayleigh + curvature) - jnp.sqrt(half * half + coupling * coupling)
    weight = energy - rayleigh
    return energy, weight, jnp.sqrt(coupling * coupling + weight * weight)


def finish_kernel(row_ref, coef_ref, start_ref, dir_ref, h_ref, hd_ref, pre_ref, out_ref, energy_ref):
    vecs, blocks = out_ref.shape[:2]
    chains = [row_ref[i] for i in range(16)]
    for i in range(16, row_ref.shape[0]):
        chains[i % 16] = chains[i % 16] + row_ref[i]
    while len(chains) > 1:
        chains = [x + y for x, y in zip(chains[::2], chains[1::2])]
    row = chains[0]
    count = len(PLAIN) + 2 * len(PAIRS) + 15
    total = [pick(row, i, vecs) for i in range(count)]
    one = {p: total[i] for i, p in enumerate(PLAIN)}
    first = {p: total[len(PLAIN) + i] for i, p in enumerate(PAIRS)}
    second = {p: total[len(PLAIN) + len(PAIRS) + i] for i, p in enumerate(PAIRS)}
    far = total[len(PLAIN) + 2 * len(PAIRS) :]
    old_ray, old_corr, _, scale, coupling, old_norm = [coef_ref[j, 0:1] for j in range(6)]

    _, weight, size = lowest(old_ray, one[(1, 3)], coupling)
    keep, mix = coupling / size, weight / size
    v_of, h_of = [(0, keep), (1, mix)], [(2, keep), (3, mix)]
    rayleigh = form(one, v_of, h_of)
    resid_of = h_of + [(i, -rayleigh * x) for i, x in v_of]
    correlation = form(first, v_of, resid_of)
    square = form(second, resid_of, resid_of) - 2.0 * correlation * form(first, v_of, resid_of)
    square = square + correlation * correlation * form(one, v_of, v_of)
    norm = jnp.sqrt(jnp.maximum(square, 0.0) + 1e-06)
    coupling = (form(first, resid_of, h_of) - correlation * rayleigh) / norm

    mult = [
        mix,
        scale * keep * (old_ray - rayleigh),
        -rayleigh * mix,
        keep * old_norm - correlation * mix,
        scale * keep * (old_corr - correlation),
    ]
    back = 1.0 / scale
    on_hd = far[:5]
    on_start = [far[5]] + [far[7 + i] for i in range(4)]
    on_dir = [far[6]] + [far[11 + i] for i in range(4)]
    on_d = [first[3, 3], first[0, 3] * back, first[1, 3], one[1, 3], one[0, 3] * back]
    on_v = [first[2, 3], first[0, 2] * back, first[1, 2], one[1, 2], one[0, 2] * back]
    curvature = None
    for j, column in enumerate([on_hd, on_start, on_dir, on_d, on_v]):
        line = None
        for i in range(5):
            term = mult[i] * column[i]
            line = term if line is None else line + term
        line = line * (mult[j] * back if j == 4 else mult[j])
        curvature = line if curvature is None else curvature + line
    curvature = curvature / (norm * norm)
    energy, weight, size = lowest(rayleigh, curvature, coupling)
    of_v, of_raw = coupling / size, weight / (norm * size)
    values = (keep * scale, mix, rayleigh, correlation, of_v, of_raw)
    for u in range(vecs):
        energy_ref[u] = lane_of(energy, u)[0, 0]
        first_v, then_d, ray, corr, use_v, use_raw = [lane_of(x, u) for x in values]
        for b in range(blocks):
            new_v = first_v * start_ref[u, b].astype(F32) + then_d * dir_ref[u, b]
            new_h = first_v * h_ref[u, b] + then_d * hd_ref[u, b]
            raw = pre_ref[b] * (new_h - ray * new_v) - corr * new_v
            out_ref[u, b] = use_v * new_v + use_raw * raw


def call(kernel, outs, args, smem=0, scratch=(), flops=0, smem_outs=0, anywhere=False):
    vmem = pl.BlockSpec(memory_space=pltpu.VMEM)
    bulk = pl.BlockSpec(memory_space=pltpu.HBM) if anywhere else vmem
    specs = [pl.BlockSpec(memory_space=pltpu.SMEM)] * smem + [bulk] * (len(args) - smem)
    size = sum(x.size * x.dtype.itemsize for x in list(outs) + list(args))
    return pl.pallas_call(
        kernel,
        out_shape=[jax.ShapeDtypeStruct(x.shape, x.dtype) for x in outs],
        in_specs=specs,
        out_specs=[vmem] * (len(outs) - smem_outs)
        + [pl.BlockSpec(memory_space=pltpu.SMEM)] * smem_outs,
        scratch_shapes=scratch,
        compiler_params=pltpu.CompilerParams(vmem_limit_bytes=24 << 20),
        cost_estimate=pl.CostEstimate(flops=flops, bytes_accessed=size, transcendentals=0),
    )(*args)


def shards(start_vectors, left_env, right_env, term_shift, precond, block_dims):
    vecs, blocks, states, _ = start_vectors.shape
    groups = lax.axis_size("term")
    sec = lax.axis_size("sec")
    share = states // groups
    core_id = (lax.axis_index("sec") & 1).reshape(1)
    term_id = lax.axis_index("term").reshape(1)
    factor = 1.0 / (blocks * sec * states * states)
    shape = jax.ShapeDtypeStruct

    core_pairs = [(i, i ^ 1) for i in range(sec)]
    chip_pairs = [(i, i + 1) for i in range(1, sec - 1, 2)]
    chip_pairs = chip_pairs + [(j, i) for i, j in chip_pairs]

    def far(x):
        return lax.ppermute(x, "sec", chip_pairs)

    def near(x):
        return lax.ppermute(x, "sec", core_pairs)

    def apply_op(x, fields=(), paired=(), keep=True):
        outs = []
        if not fields:
            outs = [shape((groups, vecs, blocks, share, states), BF)]
        elif keep:
            outs = [shape((vecs, blocks, states, states), BF)]
        count = (len(fields), len(paired))
        if sum(count):
            outs.append(shape((sum(count), vecs, 8, 128), F32))
        result = call(
            functools.partial(apply_kernel, count),
            outs,
            [core_id, term_shift, x, right_all, left_here, *fields, *paired],
            smem=2,
            scratch=[pltpu.VMEM((blocks, left_env.shape[0] * states, vecs * states), BF)],
            flops=16 * vecs * blocks * states**3,
        )
        return result[0] if len(outs) == 1 else result

    def exchange(parts, axis="term"):
        return lax.all_to_all(parts, axis, 0, 0)

    barrier = lax.optimization_barrier

    slice_shape = shape((vecs, blocks, share, states), F32)
    edge_shape = shape((vecs, states, states), BF)
    four_shape = shape((vecs, 4, states, states), BF)
    lines = vecs * blocks * share
    terms = right_env.shape[0]

    def in_hbm(x):
        return pltpu.with_memory_space_constraint(x, pltpu.HBM)

    start_hbm, left_hbm, right_hbm, pre_hbm = [
        in_hbm(x) for x in (start_vectors, left_env, right_env, precond)
    ]

    (pack_chip,) = call(
        pack_kernel,
        [shape((terms + vecs, states, states), BF)],
        [core_id, in_hbm(block_dims), start_hbm, right_hbm],
        smem=1,
        scratch=[
            pltpu.SMEM(block_dims.shape, jnp.int32),
            pltpu.VMEM((vecs, states, states), BF),
            pltpu.SemaphoreType.DMA((1 + vecs + terms,)),
        ],
        anywhere=True,
    )
    pack_chip = far(pack_chip)
    start, left_here, right_here, mask_rows, pre, vec, pack_core = call(
        load_kernel,
        [
            shape(start_vectors.shape, BF),
            shape(left_env.shape, BF),
            shape(right_env.shape, BF),
            shape((blocks, share, states), F32),
            shape((blocks, share, states), F32),
            shape((vecs, blocks, share, states), BF),
            shape((terms + vecs, states, states), BF),
        ],
        [core_id, term_id, block_dims, term_shift, start_hbm, left_hbm, right_hbm, pre_hbm],
        smem=4,
        scratch=[
            pltpu.VMEM(start_vectors.shape, BF),
            pltpu.VMEM(precond.shape, F32),
            pltpu.SemaphoreType.DMA((2 + 3 * terms,)),
        ],
        anywhere=True,
    )
    pack_core = near(pack_core)
    packs = [pack_core, pack_chip]
    right_all = jnp.concatenate([right_here] + [x[:terms, None] for x in packs], axis=1)
    start_all = jnp.concatenate([start] + [x[terms:, None] for x in packs], axis=1)
    got = exchange(apply_op(start_all))
    h_raw, body = call(
        functools.partial(settle_kernel, factor),
        [slice_shape, shape((groups, lines + EXTRA, states), BF)],
        [got, mask_rows, vec, pre],
    )
    got = exchange(body)
    pack_shape = shape((vecs + 1, states, states), BF)
    inner, outer, row = call(
        unpack_kernel,
        [pack_shape, pack_shape, shape((sec, 1, 128), F32)],
        [core_id, got, precond],
        smem=1,
    )
    h_chip, h_core = far(outer), near(inner)
    packs = [h_core, h_chip]
    row = exchange(row, "sec")
    dir_all, m_dir, coef = call(
        form_kernel,
        [four_shape, four_shape, shape((6, 8, 128), F32)],
        [row, got, h_core, h_chip, start_all, precond, *packs],
    )
    parts, dir_all, m_dir = barrier((apply_op(dir_all), dir_all, m_dir))
    got = exchange(parts)
    h_dir, body = call(
        functools.partial(settle_kernel, factor),
        [slice_shape, shape((groups, lines, states), BF)],
        [got, mask_rows],
    )
    got = exchange(body)
    got, h_dir, m_dir, start_all = barrier((got, h_dir, m_dir, start_all))
    inner, outer = call(unpack_kernel, [edge_shape, edge_shape], [core_id, got], smem=1)
    hd_chip, hd_core = far(outer), near(inner)
    (m_start,) = call(lift_start_kernel, [four_shape], [start_all, precond, *packs])
    known = [m_start, m_dir, dir_all, start_all]
    h_m_start, dots_start = apply_op(m_start, known)
    h_m_dir, dots_dir = apply_op(m_dir, known)
    gram, direction = call(
        gram_kernel,
        [shape((len(PLAIN) + 2 * len(PAIRS), vecs, 8, 128), F32), slice_shape],
        [coef, vec, h_raw, h_dir, pre],
    )
    (m_hd,) = call(lift_kernel, [four_shape], [got, hd_core, hd_chip, precond, *packs])
    dots_hd = apply_op(m_hd, [m_hd] + known, [h_m_start, h_m_dir], keep=False)
    everyone = groups * sec
    (row,) = call(
        functools.partial(tally_kernel, factor),
        [shape((everyone, 1, 128), F32)],
        [gram, dots_hd, dots_start, dots_dir],
    )
    row = exchange(row, ("term", "sec"))
    final, energy = call(
        finish_kernel,
        [slice_shape, shape((vecs,), F32)],
        [row, coef, vec, direction, h_raw, h_dir, pre],
        smem_outs=1,
    )
    return (final, energy)


def solution(mesh):
    return jax.shard_map(
        shards,
        mesh=mesh,
        in_specs=(
            P(None, "sec", None, None),
            P("term", "sec", None, None),
            P("term", "sec", None, None),
            P("term"),
            P("sec", None, None),
            P("sec"),
        ),
        out_specs=(P(None, "sec", "term", None), P()),
        check_vma=False,
    )
```

profile of v0, /device:TPU:1, one launch (start us, length us, event | category | flops | bytes accessed | tf_op | source)
XLA Modules:
  0.0 158.3 jit_solution(11941271358696494494)
XLA Ops:
  0.7 1.3 shard_map.78
  1.9 4.5 %collective-permute-start.1 = (bf16[6,256,256]{2,1,0:T(8,128)(2,1)S(1)}, bf16[6,256,256]{2,1,0:T(8,128)(2,1)S(1)}, u32[]{:S(2)}, u32[]{:S(2)}) collective-permute-start(bf16[6,256,256]{2,1,0:T(8,128)(2,1)S(1)} %shard_map.78), channel_id=1, source_target_pairs={{1,2},{3,4},{5,6},{7,8},{9,10},{11,12},{13,14},{15,16},{17,18},{19... | collective-permute-start | bytes 2359304 | tf_op jit(solution)/shard_map/ppermute | solution.py:398
  6.5 2.6 %shard_map.77 = (bf16[2,2,256,256]{3,2,1,0:T(8,128)(2,1)S(1)}, bf16[4,2,256,256]{3,2,1,0:T(8,128)(2,1)S(1)}, bf16[4,2,256,256]{3,2,1,0:T(8,128)(2,1)S(1)}, f32[2...) custom-call(s32[1]{0:T(128)} %bitcast.core_ref, ...), custom_call_target="tpu_custom_call" | custom-call | bytes 6750240 | tf_op jit(solution)/shard_map/pallas_call | solution.py:371
  9.2 6.9 %collective-permute-done.1 = bf16[6,256,256]{2,1,0:T(8,128)(2,1)S(1)} collective-permute-done((bf16[6,256,256]{2,1,0:T(8,128)(2,1)S(1)}, bf16[6,256,256]{2,1,0:T(8,128)(2,1)S(1)}, u32[]{:S(2)}, u32[]{:S(2)}) %collective-permute-start.1) | collective-permute-done | bytes 786464 | tf_op jit(solution)/shard_map/ppermute | solution.py:398
  16.6 1.8 %shard_map.79 = bf16[8,2,2,32,256]{4,3,2,1,0:T(8,128)(2,1)S(1)} custom-call(s32[1]{0:T(128)} %bitcast.core_ref, s32[4]{0:T(128)S(1)} %copy-done.1, bf16[2,4,256,256]{3,2,1,0:T(8,128)(2,1)S(1)} %pad_maximum_fusion.1.x_ref.start_ref.refs_3_.refs_4_, bf16[4,4,256,256]{3,2,1,0:T(8,128)(2,1)S(1)} %pad_maximum_fusion.right_ref, ...), custom_call_target="tpu_custom_call" | custom-call | flops 1073741824 | bytes 4718612 | tf_op jit(solution)/shard_map/pallas_call | solution.py:371
  18.5 22.1 %all_to_all.30.got_ref = bf16[8,2,2,32,256]{4,3,2,1,0:T(8,128)(2,1)S(1)} all-to-all(bf16[8,2,2,32,256]{4,3,2,1,0:T(8,128)(2,1)S(1)} %shard_map.79), channel_id=1, replica_groups=mesh['term'=8,'sec'=32] {'term'}, dimensions={0} | all-to-all | bytes 1048576 | tf_op jit(solution)/shard_map/all_to_all | solution.py:423
  40.6 0.3 shard_map.80
  40.9 19.7 %all_to_all.31.got_ref = bf16[8,136,256]{2,1,0:T(8,128)(2,1)S(1)} all-to-all(bf16[8,136,256]{2,1,0:T(8,128)(2,1)S(1)} %get-tuple-element.41), channel_id=1, replica_groups=mesh['term'=8,'sec'=32] {'term'}, dimensions={0} | all-to-all | bytes 1114112 | tf_op jit(solution)/shard_map/all_to_all | solution.py:423
  60.7 7.8 %collective-permute-start.3 = (bf16[3,256,256]{2,1,0:T(8,128)(2,1)S(1)}, bf16[3,256,256]{2,1,0:T(8,128)(2,1)S(1)}, u32[]{:S(2)}, u32[]{:S(2)}) collective-permute-start(bf16[3,256,256]{2,1,0:T(8,128)(2,1)S(1)} %get-tuple-element.44), channel_id=1, source_target_pairs={{1,2},{3,4},{5,6},{7,8},{9,10},{11,12},{13,14},{15,16},{17,18},{19... | collective-permute-start | bytes 1179656 | tf_op jit(solution)/shard_map/ppermute | solution.py:398
  68.5 16.0 %all_to_all.32.row_ref = f32[32,1,128]{2,1,0:T(1,128)S(1)} all-to-all(f32[32,1,128]{2,1,0:T(1,128)S(1)} %get-tuple-element.42), channel_id=1, replica_groups=mesh['term'=8,'sec'=32] {'sec'}, dimensions={0} | all-to-all | bytes 32768 | tf_op jit(solution)/shard_map/all_to_all | solution.py:423
  84.5 1.5 shard_map.82
  86.0 1.8 %shard_map.83 = bf16[8,2,2,32,256]{4,3,2,1,0:T(8,128)(2,1)S(1)} custom-call(s32[1]{0:T(128)} %bitcast.core_ref, s32[4]{0:T(128)S(1)} %copy-done.1, bf16[2,4,256,256]{3,2,1,0:T(8,128)(2,1)S(1)} %get-tuple-element.60.x_ref.refs_2_.refs_3_, bf16[4,4,256,256]{3,2,1,0:T(8,128)(2,1)S(1)} %pad_maximum_fusion.right_ref, ...), custom_call_target="tpu_custom_call" | custom-call | flops 1073741824 | bytes 4718612 | tf_op jit(solution)/shard_map/pallas_call | solution.py:371
  87.8 19.1 %all_to_all.33.got_ref = bf16[8,2,2,32,256]{4,3,2,1,0:T(8,128)(2,1)S(1)} all-to-all(bf16[8,2,2,32,256]{4,3,2,1,0:T(8,128)(2,1)S(1)} %shard_map.83), channel_id=1, replica_groups=mesh['term'=8,'sec'=32] {'term'}, dimensions={0} | all-to-all | bytes 1048576 | tf_op jit(solution)/shard_map/all_to_all | solution.py:423
  107.1 17.5 %all_to_all.34.got_ref = bf16[8,128,256]{2,1,0:T(8,128)(2,1)S(1)} all-to-all(bf16[8,128,256]{2,1,0:T(8,128)(2,1)S(1)} %get-tuple-element.50), channel_id=1, replica_groups=mesh['term'=8,'sec'=32] {'term'}, dimensions={0} | all-to-all | bytes 1048576 | tf_op jit(solution)/shard_map/all_to_all | solution.py:423
  124.7 3.4 %collective-permute-start.4 = (bf16[2,256,256]{2,1,0:T(8,128)(2,1)S(1)}, bf16[2,256,256]{2,1,0:T(8,128)(2,1)S(1)}, u32[]{:S(2)}, u32[]{:S(2)}) collective-permute-start(bf16[2,256,256]{2,1,0:T(8,128)(2,1)S(1)} %get-tuple-element.56), channel_id=1, source_target_pairs={{0,1},{1,0},{2,3},{3,2},{4,5},{5,4},{6,7},{7,6},{8,9},{9,8},{10,11... | collective-permute-start | bytes 786440 | tf_op jit(solution)/shard_map/ppermute | solution.py:401
  128.1 2.3 %collective-permute-start.5 = (bf16[2,256,256]{2,1,0:T(8,128)(2,1)S(1)}, bf16[2,256,256]{2,1,0:T(8,128)(2,1)S(1)}, u32[]{:S(2)}, u32[]{:S(2)}) collective-permute-start(bf16[2,256,256]{2,1,0:T(8,128)(2,1)S(1)} %get-tuple-element.57), channel_id=1, source_target_pairs={{1,2},{3,4},{5,6},{7,8},{9,10},{11,12},{13,14},{15,16},{17,18},{19... | collective-permute-start | bytes 786440 | tf_op jit(solution)/shard_map/ppermute | solution.py:398
  130.4 0.5 shard_map.85
  131.1 2.1 %shard_map.90 = (bf16[2,2,256,256]{3,2,1,0:T(8,128)(2,1)S(1)}, f32[4,2,8,128]{3,2,1,0:T(8,128)S(1)}) custom-call(s32[1]{0:T(128)} %bitcast.core_ref, s32[4]{0:T(128)S(1)} %copy-done.1, bf16[2,4,256,256]{3,2,1,0:T(8,128)(2,1)S(1)} %get-tuple-element.59.refs_1_.x_ref.refs_2_, bf16[4,4,256,256]{3,2,1,0:T(8,128)(2,1)S(1)} %pad_maximum_fusion.right_ref, ...), custom_call_target="tpu_custom_call" | custom-call | flops 1073741824 | bytes 8945684 | tf_op jit(solution)/shard_map/pallas_call | solution.py:371
  133.2 2.1 %shard_map.89 = (bf16[2,2,256,256]{3,2,1,0:T(8,128)(2,1)S(1)}, f32[4,2,8,128]{3,2,1,0:T(8,128)S(1)}) custom-call(s32[1]{0:T(128)} %bitcast.core_ref, s32[4]{0:T(128)S(1)} %copy-done.1, bf16[2,4,256,256]{3,2,1,0:T(8,128)(2,1)S(1)} %shard_map.88.x_ref.refs_0_.refs_1_, bf16[4,4,256,256]{3,2,1,0:T(8,128)(2,1)S(1)} %pad_maximum_fusion.right_ref, ...), custom_call_target="tpu_custom_call" | custom-call | flops 1073741824 | bytes 8945684 | tf_op jit(solution)/shard_map/pallas_call | solution.py:371
  135.3 0.4 collective-permute-done.5.chip_ref
  136.0 2.3 %shard_map.91.refs_1_ = f32[7,2,8,128]{3,2,1,0:T(8,128)S(1)} custom-call(s32[1]{0:T(128)} %bitcast.core_ref, s32[4]{0:T(128)S(1)} %copy-done.1, bf16[2,4,256,256]{3,2,1,0:T(8,128)(2,1)S(1)} %shard_map.87.x_ref.refs_0_, bf16[4,4,256,256]{3,2,1,0:T(8,128)(2,1)S(1)} %pad_maximum_fusion.right_ref, bf16[4,2,256,256]{3,2,1,0:T(8,128)(2,1)S(1)} %get-tuple-element.37.left_ref, ...), custom_call_target="tpu_custom_call" | custom-call | flops 1073741824 | bytes 10543124 | tf_op jit(solution)/shard_map/pallas_call | solution.py:371
  138.2 0.3 shard_map.92
  138.6 18.5 %all_to_all.35.row_ref = f32[256,1,128]{2,1,0:T(1,128)S(1)} all-to-all(f32[256,1,128]{2,1,0:T(1,128)S(1)} %shard_map.92), channel_id=1, replica_groups=mesh['term'=8,'sec'=32] {'term','sec'}, dimensions={0} | all-to-all | bytes 262144 | tf_op jit(solution)/shard_map/all_to_all | solution.py:423
  157.1 1.0 shard_map.93
  (23 shorter events, 1.3 us)
Async XLA Ops:
  0.6 5.8 %copy-start.2 = (s32[2]{0:T(128)S(1)}, s32[2]{0:T(128)}, u32[]{:S(2)}) copy-start(s32[2]{0:T(128)} %dims_hbm.1) | copy-start | bytes 28
  0.6 5.8 %copy-start.1 = (s32[4]{0:T(128)S(1)}, s32[4]{0:T(128)}, u32[]{:S(2)}) copy-start(s32[4]{0:T(128)} %shift_ref.11) | copy-start | bytes 52
  1.9 14.2 %collective-permute-start.1 = (bf16[6,256,256]{2,1,0:T(8,128)(2,1)S(1)}, bf16[6,256,256]{2,1,0:T(8,128)(2,1)S(1)}, u32[]{:S(2)}, u32[]{:S(2)}) collective-permute-start(bf16[6,256,256]{2,1,0:T(8,128)(2,1)S(1)} %shard_map.78), channel_id=1, source_target_pairs={{1,2},{3,4},{5,6},{7,8},{9,10},{11,12},{13,14},{15,16},{17,18},{19... | collective-permute-start | bytes 2359304 | tf_op jit(solution)/shard_map/ppermute | solution.py:398
  9.1 7.0 %collective-permute-start = (bf16[6,256,256]{2,1,0:T(8,128)(2,1)S(1)}, bf16[6,256,256]{2,1,0:T(8,128)(2,1)S(1)}, u32[]{:S(2)}, u32[]{:S(2)}) collective-permute-start(bf16[6,256,256]{2,1,0:T(8,128)(2,1)S(1)} %get-tuple-element.35), channel_id=1, source_target_pairs={{0,1},{1,0},{2,3},{3,2},{4,5},{5,4},{6,7},{7,6},{8,9},{9,8},{10,11... | collective-permute-start | bytes 2359304 | tf_op jit(solution)/shard_map/ppermute | solution.py:401
  18.5 42.1 %copy-start = (f32[2,256,256]{2,1,0:T(8,128)S(1)}, f32[2,256,256]{2,1,0:T(8,128)}, u32[]{:S(2)}) copy-start(f32[2,256,256]{2,1,0:T(8,128)} %pre_ref.7) | copy-start | bytes 1572868
  60.6 23.9 %collective-permute-start.2 = (bf16[3,256,256]{2,1,0:T(8,128)(2,1)S(1)}, bf16[3,256,256]{2,1,0:T(8,128)(2,1)S(1)}, u32[]{:S(2)}, u32[]{:S(2)}) collective-permute-start(bf16[3,256,256]{2,1,0:T(8,128)(2,1)S(1)} %get-tuple-element.43), channel_id=1, source_target_pairs={{0,1},{1,0},{2,3},{3,2},{4,5},{5,4},{6,7},{7,6},{8,9},{9,8},{10,11... | collective-permute-start | bytes 1179656 | tf_op jit(solution)/shard_map/ppermute | solution.py:401
  60.7 23.8 %collective-permute-start.3 = (bf16[3,256,256]{2,1,0:T(8,128)(2,1)S(1)}, bf16[3,256,256]{2,1,0:T(8,128)(2,1)S(1)}, u32[]{:S(2)}, u32[]{:S(2)}) collective-permute-start(bf16[3,256,256]{2,1,0:T(8,128)(2,1)S(1)} %get-tuple-element.44), channel_id=1, source_target_pairs={{1,2},{3,4},{5,6},{7,8},{9,10},{11,12},{13,14},{15,16},{17,18},{19... | collective-permute-start | bytes 1179656 | tf_op jit(solution)/shard_map/ppermute | solution.py:398
  124.7 10.6 %collective-permute-start.4 = (bf16[2,256,256]{2,1,0:T(8,128)(2,1)S(1)}, bf16[2,256,256]{2,1,0:T(8,128)(2,1)S(1)}, u32[]{:S(2)}, u32[]{:S(2)}) collective-permute-start(bf16[2,256,256]{2,1,0:T(8,128)(2,1)S(1)} %get-tuple-element.56), channel_id=1, source_target_pairs={{0,1},{1,0},{2,3},{3,2},{4,5},{5,4},{6,7},{7,6},{8,9},{9,8},{10,11... | collective-permute-start | bytes 786440 | tf_op jit(solution)/shard_map/ppermute | solution.py:401
  128.1 7.7 %collective-permute-start.5 = (bf16[2,256,256]{2,1,0:T(8,128)(2,1)S(1)}, bf16[2,256,256]{2,1,0:T(8,128)(2,1)S(1)}, u32[]{:S(2)}, u32[]{:S(2)}) collective-permute-start(bf16[2,256,256]{2,1,0:T(8,128)(2,1)S(1)} %get-tuple-element.57), channel_id=1, source_target_pairs={{1,2},{3,4},{5,6},{7,8},{9,10},{11,12},{13,14},{15,16},{17,18},{19... | collective-permute-start | bytes 786440 | tf_op jit(solution)/shard_map/ppermute | solution.py:398
where the time goes:
time: 159 us; the launch traced here: 158 us
  blocking collectives  113 us (71%)
  Pallas kernels  18.3 us (12%)
  starting transfers between devices  18.2 us (11%)
  waiting for transfers between devices  7.33 us (5%)
    all_to_all x6, blocking collectives, exchange(): return lax.all_to_all(parts, axis, 0, 0)  113 us
    pallas_call x17, Pallas kernels, call(): pl.pallas_call(kernel, out_shape=[jax.ShapeDtypeStruct(x.shape, x.dtype)...  18.3 us
    ppermute x3, starting transfers between devices, far(): return lax.ppermute(x, 'sec', chip_pairs)  14.6 us
    ppermute x3, waiting for transfers between devices, far(): return lax.ppermute(x, 'sec', chip_pairs)  7.32 us
    ppermute x3, starting transfers between devices, near(): return lax.ppermute(x, 'sec', core_pairs)  3.58 us
  transfers between devices with their start and end apart: 6, of which 2 were waited for; matrix products, arithmetic and copies ran while one was open for 0% of the time, Pallas kernels for 5%

commit v1 on v0

--- a/solution.py
+++ b/solution.py
@@ -12,7 +12,7 @@
 F32 = jnp.float32
 PAIRS = [(i, j) for i in range(4) for j in range(i, 4)]
 PLAIN = [(0, 0), (0, 1), (1, 1), (0, 2), (0, 3), (1, 2), (1, 3)]
-EXTRA = 8
+EXTRA = 16
 
 
 def fold(product):
@@ -146,7 +146,7 @@
     return ref[ref.shape[0] - 1].astype(F32)
 
 
-def form_kernel(row_ref, got_ref, core_ref, chip_ref, start_ref, pre_ref, pre_core, pre_chip, dir_ref, mdir_ref, coef_ref):
+def form_kernel(row_ref, got_ref, core_ref, chip_ref, start_ref, pre_ref, pre_core, pre_chip, dir_ref, coef_ref):
     vecs, slots, states, _ = dir_ref.shape
     share = states // got_ref.shape[0]
     row = row_ref[0]
@@ -170,9 +170,7 @@
             m = weight_of(pre_ref, pre_core, pre_chip, i)
             v = start_ref[u, i].astype(F32)
             raw = m * (hs[i].astype(F32) - ray * v) - corr * v
-            small = (raw * mult).astype(BF)
-            dir_ref[u, i] = small
-            mdir_ref[u, i] = (m * small.astype(F32)).astype(BF)
+            dir_ref[u, i] = (raw * mult).astype(BF)
 
 
 def lift_kernel(got_ref, core_ref, chip_ref, pre_ref, pre_core, pre_chip, out_ref):
@@ -491,12 +489,12 @@
     h_chip, h_core = far(outer), near(inner)
     packs = [h_core, h_chip]
     row = exchange(row, "sec")
-    dir_all, m_dir, coef = call(
+    dir_all, coef = call(
         form_kernel,
-        [four_shape, four_shape, shape((6, 8, 128), F32)],
+        [four_shape, shape((6, 8, 128), F32)],
         [row, got, h_core, h_chip, start_all, precond, *packs],
     )
-    parts, dir_all, m_dir = barrier((apply_op(dir_all), dir_all, m_dir))
+    parts, dir_all = barrier((apply_op(dir_all), dir_all))
     got = exchange(parts)
     h_dir, body = call(
         functools.partial(settle_kernel, factor),
@@ -504,10 +502,11 @@
         [got, mask_rows],
     )
     got = exchange(body)
-    got, h_dir, m_dir, start_all = barrier((got, h_dir, m_dir, start_all))
+    got, h_dir, dir_all, start_all = barrier((got, h_dir, dir_all, start_all))
     inner, outer = call(unpack_kernel, [edge_shape, edge_shape], [core_id, got], smem=1)
     hd_chip, hd_core = far(outer), near(inner)
     (m_start,) = call(lift_start_kernel, [four_shape], [start_all, precond, *packs])
+    (m_dir,) = call(lift_start_kernel, [four_shape], [dir_all, precond, *packs])
     known = [m_start, m_dir, dir_all, start_all]
     h_m_start, dots_start = apply_op(m_start, known)
     h_m_dir, dots_dir = apply_op(m_dir, known)

time: 159 us -> 159 us (level)
    pallas_call x17 -> x18, Pallas kernels: 18.3 us -> 18.2 us  [call(): pl.pallas_call(kernel, out_shape=[jax.ShapeDtypeStruct(x.shape, x.dtype)...]
where the time goes in v1:
time: 159 us
  blocking collectives  114 us (72%)
  Pallas kernels  18.2 us (11%)
  starting transfers between devices  18.2 us (11%)
  waiting for transfers between devices  7.07 us (4%)
    all_to_all x6, blocking collectives, exchange(): return lax.all_to_all(parts, axis, 0, 0)  114 us
    pallas_call x18, Pallas kernels, call(): pl.pallas_call(kernel, out_shape=[jax.ShapeDtypeStruct(x.shape, x.dtype)...  18.2 us
    ppermute x3, starting transfers between devices, far(): return lax.ppermute(x, 'sec', chip_pairs)  14.6 us
    ppermute x3, waiting for transfers between devices, far(): return lax.ppermute(x, 'sec', chip_pairs)  7.07 us
    ppermute x3, starting transfers between devices, near(): return lax.ppermute(x, 'sec', core_pairs)  3.58 us
  transfers between devices with their start and end apart: 6, of which 2 were waited for; matrix products, arithmetic and copies ran while one was open for 0% of the time, Pallas kernels for 5%

profile of v1, /device:TPU:1, one launch (start us, length us, event | category | flops | bytes accessed | tf_op | source)
XLA Modules:
  0.0 158.9 jit_solution(18005728575117321171)
XLA Ops:
  0.7 1.3 shard_map.78
  1.9 4.5 %collective-permute-start.1 = (bf16[6,256,256]{2,1,0:T(8,128)(2,1)S(1)}, bf16[6,256,256]{2,1,0:T(8,128)(2,1)S(1)}, u32[]{:S(2)}, u32[]{:S(2)}) collective-permute-start(bf16[6,256,256]{2,1,0:T(8,128)(2,1)S(1)} %shard_map.78), channel_id=1, source_target_pairs={{1,2},{3,4},{5,6},{7,8},{9,10},{11,12},{13,14},{15,16},{17,18},{19... | collective-permute-start | bytes 2359304 | tf_op jit(solution)/shard_map/ppermute | solution.py:396
  6.5 2.6 %shard_map.77 = (bf16[2,2,256,256]{3,2,1,0:T(8,128)(2,1)S(1)}, bf16[4,2,256,256]{3,2,1,0:T(8,128)(2,1)S(1)}, bf16[4,2,256,256]{3,2,1,0:T(8,128)(2,1)S(1)}, f32[2...) custom-call(s32[1]{0:T(128)} %bitcast.core_ref, ...), custom_call_target="tpu_custom_call" | custom-call | bytes 6750240 | tf_op jit(solution)/shard_map/pallas_call | solution.py:369
  9.2 6.9 %collective-permute-done.1 = bf16[6,256,256]{2,1,0:T(8,128)(2,1)S(1)} collective-permute-done((bf16[6,256,256]{2,1,0:T(8,128)(2,1)S(1)}, bf16[6,256,256]{2,1,0:T(8,128)(2,1)S(1)}, u32[]{:S(2)}, u32[]{:S(2)}) %collective-permute-start.1) | collective-permute-done | bytes 786464 | tf_op jit(solution)/shard_map/ppermute | solution.py:396
  16.6 1.8 %shard_map.79 = bf16[8,2,2,32,256]{4,3,2,1,0:T(8,128)(2,1)S(1)} custom-call(s32[1]{0:T(128)} %bitcast.core_ref, s32[4]{0:T(128)S(1)} %copy-done.1, bf16[2,4,256,256]{3,2,1,0:T(8,128)(2,1)S(1)} %pad_maximum_fusion.1.x_ref.start_ref.refs_3_.refs_4_, bf16[4,4,256,256]{3,2,1,0:T(8,128)(2,1)S(1)} %pad_maximum_fusion.right_ref, ...), custom_call_target="tpu_custom_call" | custom-call | flops 1073741824 | bytes 4718612 | tf_op jit(solution)/shard_map/pallas_call | solution.py:369
  18.5 22.1 %all_to_all.30.got_ref = bf16[8,2,2,32,256]{4,3,2,1,0:T(8,128)(2,1)S(1)} all-to-all(bf16[8,2,2,32,256]{4,3,2,1,0:T(8,128)(2,1)S(1)} %shard_map.79), channel_id=1, replica_groups=mesh['term'=8,'sec'=32] {'term'}, dimensions={0} | all-to-all | bytes 1048576 | tf_op jit(solution)/shard_map/all_to_all | solution.py:421
  40.6 0.3 shard_map.80
  40.9 20.4 %all_to_all.31.got_ref = bf16[8,144,256]{2,1,0:T(8,128)(2,1)S(1)} all-to-all(bf16[8,144,256]{2,1,0:T(8,128)(2,1)S(1)} %get-tuple-element.39), channel_id=1, replica_groups=mesh['term'=8,'sec'=32] {'term'}, dimensions={0} | all-to-all | bytes 1179648 | tf_op jit(solution)/shard_map/all_to_all | solution.py:421
  61.4 7.8 %collective-permute-start.3 = (bf16[3,256,256]{2,1,0:T(8,128)(2,1)S(1)}, bf16[3,256,256]{2,1,0:T(8,128)(2,1)S(1)}, u32[]{:S(2)}, u32[]{:S(2)}) collective-permute-start(bf16[3,256,256]{2,1,0:T(8,128)(2,1)S(1)} %get-tuple-element.42), channel_id=1, source_target_pairs={{1,2},{3,4},{5,6},{7,8},{9,10},{11,12},{13,14},{15,16},{17,18},{19... | collective-permute-start | bytes 1179656 | tf_op jit(solution)/shard_map/ppermute | solution.py:396
  69.2 16.0 %all_to_all.32.row_ref = f32[32,1,128]{2,1,0:T(1,128)S(1)} all-to-all(f32[32,1,128]{2,1,0:T(1,128)S(1)} %get-tuple-element.40), channel_id=1, replica_groups=mesh['term'=8,'sec'=32] {'sec'}, dimensions={0} | all-to-all | bytes 32768 | tf_op jit(solution)/shard_map/all_to_all | solution.py:421
  85.2 1.2 shard_map.82
  86.4 1.8 %shard_map.83 = bf16[8,2,2,32,256]{4,3,2,1,0:T(8,128)(2,1)S(1)} custom-call(s32[1]{0:T(128)} %bitcast.core_ref, s32[4]{0:T(128)S(1)} %copy-done.1, bf16[2,4,256,256]{3,2,1,0:T(8,128)(2,1)S(1)} %get-tuple-element.56.x_ref.start_ref.refs_2_.refs_3_, bf16[4,4,256,256]{3,2,1,0:T(8,128)(2,1)S(1)} %pad_maximum_fusion.right_ref, ...), custom_call_target="tpu_custom_call" | custom-call | flops 1073741824 | bytes 4718612 | tf_op jit(solution)/shard_map/pallas_call | solution.py:369
  88.2 19.1 %all_to_all.33.got_ref = bf16[8,2,2,32,256]{4,3,2,1,0:T(8,128)(2,1)S(1)} all-to-all(bf16[8,2,2,32,256]{4,3,2,1,0:T(8,128)(2,1)S(1)} %shard_map.83), channel_id=1, replica_groups=mesh['term'=8,'sec'=32] {'term'}, dimensions={0} | all-to-all | bytes 1048576 | tf_op jit(solution)/shard_map/all_to_all | solution.py:421
  107.5 17.5 %all_to_all.34.got_ref = bf16[8,128,256]{2,1,0:T(8,128)(2,1)S(1)} all-to-all(bf16[8,128,256]{2,1,0:T(8,128)(2,1)S(1)} %get-tuple-element.47), channel_id=1, replica_groups=mesh['term'=8,'sec'=32] {'term'}, dimensions={0} | all-to-all | bytes 1048576 | tf_op jit(solution)/shard_map/all_to_all | solution.py:421
  125.1 3.4 %collective-permute-start.4 = (bf16[2,256,256]{2,1,0:T(8,128)(2,1)S(1)}, bf16[2,256,256]{2,1,0:T(8,128)(2,1)S(1)}, u32[]{:S(2)}, u32[]{:S(2)}) collective-permute-start(bf16[2,256,256]{2,1,0:T(8,128)(2,1)S(1)} %get-tuple-element.53), channel_id=1, source_target_pairs={{0,1},{1,0},{2,3},{3,2},{4,5},{5,4},{6,7},{7,6},{8,9},{9,8},{10,11... | collective-permute-start | bytes 786440 | tf_op jit(solution)/shard_map/ppermute | solution.py:399
  128.4 2.3 %collective-permute-start.5 = (bf16[2,256,256]{2,1,0:T(8,128)(2,1)S(1)}, bf16[2,256,256]{2,1,0:T(8,128)(2,1)S(1)}, u32[]{:S(2)}, u32[]{:S(2)}) collective-permute-start(bf16[2,256,256]{2,1,0:T(8,128)(2,1)S(1)} %get-tuple-element.54), channel_id=1, source_target_pairs={{1,2},{3,4},{5,6},{7,8},{9,10},{11,12},{13,14},{15,16},{17,18},{19... | collective-permute-start | bytes 786440 | tf_op jit(solution)/shard_map/ppermute | solution.py:396
  130.8 0.5 shard_map.85
  131.7 2.1 %shard_map.91 = (bf16[2,2,256,256]{3,2,1,0:T(8,128)(2,1)S(1)}, f32[4,2,8,128]{3,2,1,0:T(8,128)S(1)}) custom-call(s32[1]{0:T(128)} %bitcast.core_ref, s32[4]{0:T(128)S(1)} %copy-done.1, bf16[2,4,256,256]{3,2,1,0:T(8,128)(2,1)S(1)} %shard_map.89.refs_1_.x_ref.refs_2_, bf16[4,4,256,256]{3,2,1,0:T(8,128)(2,1)S(1)} %pad_maximum_fusion.right_ref, ...), custom_call_target="tpu_custom_call" | custom-call | flops 1073741824 | bytes 8945684 | tf_op jit(solution)/shard_map/pallas_call | solution.py:369
  133.8 2.1 %shard_map.90 = (bf16[2,2,256,256]{3,2,1,0:T(8,128)(2,1)S(1)}, f32[4,2,8,128]{3,2,1,0:T(8,128)S(1)}) custom-call(s32[1]{0:T(128)} %bitcast.core_ref, s32[4]{0:T(128)S(1)} %copy-done.1, bf16[2,4,256,256]{3,2,1,0:T(8,128)(2,1)S(1)} %shard_map.88.x_ref.refs_0_.refs_1_, bf16[4,4,256,256]{3,2,1,0:T(8,128)(2,1)S(1)} %pad_maximum_fusion.right_ref, ...), custom_call_target="tpu_custom_call" | custom-call | flops 1073741824 | bytes 8945684 | tf_op jit(solution)/shard_map/pallas_call | solution.py:369
  136.1 0.2 shard_map.87.x_ref.refs_0_
  136.4 2.3 %shard_map.92.refs_1_ = f32[7,2,8,128]{3,2,1,0:T(8,128)S(1)} custom-call(s32[1]{0:T(128)} %bitcast.core_ref, s32[4]{0:T(128)S(1)} %copy-done.1, bf16[2,4,256,256]{3,2,1,0:T(8,128)(2,1)S(1)} %shard_map.87.x_ref.refs_0_, bf16[4,4,256,256]{3,2,1,0:T(8,128)(2,1)S(1)} %pad_maximum_fusion.right_ref, bf16[4,2,256,256]{3,2,1,0:T(8,128)(2,1)S(1)} %get-tuple-element.35.left_ref, ...), custom_call_target="tpu_custom_call" | custom-call | flops 1073741824 | bytes 10543124 | tf_op jit(solution)/shard_map/pallas_call | solution.py:369
  138.6 0.3 shard_map.93
  139.0 18.8 %all_to_all.35.row_ref = f32[256,1,128]{2,1,0:T(1,128)S(1)} all-to-all(f32[256,1,128]{2,1,0:T(1,128)S(1)} %shard_map.93), channel_id=1, replica_groups=mesh['term'=8,'sec'=32] {'term','sec'}, dimensions={0} | all-to-all | bytes 262144 | tf_op jit(solution)/shard_map/all_to_all | solution.py:421
  157.7 1.0 shard_map.94
  (24 shorter events, 1.5 us)
Async XLA Ops:
  0.6 5.8 %copy-start.2 = (s32[2]{0:T(128)S(1)}, s32[2]{0:T(128)}, u32[]{:S(2)}) copy-start(s32[2]{0:T(128)} %dims_hbm.1) | copy-start | bytes 28
  0.6 5.8 %copy-start.1 = (s32[4]{0:T(128)S(1)}, s32[4]{0:T(128)}, u32[]{:S(2)}) copy-start(s32[4]{0:T(128)} %shift_ref.11) | copy-start | bytes 52
  1.9 14.2 %collective-permute-start.1 = (bf16[6,256,256]{2,1,0:T(8,128)(2,1)S(1)}, bf16[6,256,256]{2,1,0:T(8,128)(2,1)S(1)}, u32[]{:S(2)}, u32[]{:S(2)}) collective-permute-start(bf16[6,256,256]{2,1,0:T(8,128)(2,1)S(1)} %shard_map.78), channel_id=1, source_target_pairs={{1,2},{3,4},{5,6},{7,8},{9,10},{11,12},{13,14},{15,16},{17,18},{19... | collective-permute-start | bytes 2359304 | tf_op jit(solution)/shard_map/ppermute | solution.py:396
  9.1 7.0 %collective-permute-start = (bf16[6,256,256]{2,1,0:T(8,128)(2,1)S(1)}, bf16[6,256,256]{2,1,0:T(8,128)(2,1)S(1)}, u32[]{:S(2)}, u32[]{:S(2)}) collective-permute-start(bf16[6,256,256]{2,1,0:T(8,128)(2,1)S(1)} %get-tuple-element.33), channel_id=1, source_target_pairs={{0,1},{1,0},{2,3},{3,2},{4,5},{5,4},{6,7},{7,6},{8,9},{9,8},{10,11... | collective-permute-start | bytes 2359304 | tf_op jit(solution)/shard_map/ppermute | solution.py:399
  18.5 42.8 %copy-start = (f32[2,256,256]{2,1,0:T(8,128)S(1)}, f32[2,256,256]{2,1,0:T(8,128)}, u32[]{:S(2)}) copy-start(f32[2,256,256]{2,1,0:T(8,128)} %pre_ref.9) | copy-start | bytes 1572868
  61.3 23.9 %collective-permute-start.2 = (bf16[3,256,256]{2,1,0:T(8,128)(2,1)S(1)}, bf16[3,256,256]{2,1,0:T(8,128)(2,1)S(1)}, u32[]{:S(2)}, u32[]{:S(2)}) collective-permute-start(bf16[3,256,256]{2,1,0:T(8,128)(2,1)S(1)} %get-tuple-element.41), channel_id=1, source_target_pairs={{0,1},{1,0},{2,3},{3,2},{4,5},{5,4},{6,7},{7,6},{8,9},{9,8},{10,11... | collective-permute-start | bytes 1179656 | tf_op jit(solution)/shard_map/ppermute | solution.py:399
  61.4 23.8 %collective-permute-start.3 = (bf16[3,256,256]{2,1,0:T(8,128)(2,1)S(1)}, bf16[3,256,256]{2,1,0:T(8,128)(2,1)S(1)}, u32[]{:S(2)}, u32[]{:S(2)}) collective-permute-start(bf16[3,256,256]{2,1,0:T(8,128)(2,1)S(1)} %get-tuple-element.42), channel_id=1, source_target_pairs={{1,2},{3,4},{5,6},{7,8},{9,10},{11,12},{13,14},{15,16},{17,18},{19... | collective-permute-start | bytes 1179656 | tf_op jit(solution)/shard_map/ppermute | solution.py:396
  125.1 10.9 %collective-permute-start.4 = (bf16[2,256,256]{2,1,0:T(8,128)(2,1)S(1)}, bf16[2,256,256]{2,1,0:T(8,128)(2,1)S(1)}, u32[]{:S(2)}, u32[]{:S(2)}) collective-permute-start(bf16[2,256,256]{2,1,0:T(8,128)(2,1)S(1)} %get-tuple-element.53), channel_id=1, source_target_pairs={{0,1},{1,0},{2,3},{3,2},{4,5},{5,4},{6,7},{7,6},{8,9},{9,8},{10,11... | collective-permute-start | bytes 786440 | tf_op jit(solution)/shard_map/ppermute | solution.py:399
  128.4 7.7 %collective-permute-start.5 = (bf16[2,256,256]{2,1,0:T(8,128)(2,1)S(1)}, bf16[2,256,256]{2,1,0:T(8,128)(2,1)S(1)}, u32[]{:S(2)}, u32[]{:S(2)}) collective-permute-start(bf16[2,256,256]{2,1,0:T(8,128)(2,1)S(1)} %get-tuple-element.54), channel_id=1, source_target_pairs={{1,2},{3,4},{5,6},{7,8},{9,10},{11,12},{13,14},{15,16},{17,18},{19... | collective-permute-start | bytes 786440 | tf_op jit(solution)/shard_map/ppermute | solution.py:396
